TPU v7x, 32 devices: a whole 2x2x4 slice. The times are simulated.
32 devices in a mesh: samp: 4 (over x, core), bin: 8 (over z, y).
Axes of the slice: x: 2, y: 2, z: 4, core: 2. Of those that a mesh axis runs over, the one named last changes fastest.
Arguments:
- read_depth: bfloat16 [32768, 4096], P('samp', 'bin'), may hold values from -18 to 18
- gc_weight: float32 [4096], replicated, may hold values from 0.3 to 3
- map_weight: float32 [4096], replicated, may hold values from 0.3 to 3
- kernel: float32 [33], replicated, may hold values from 0.2 to 1
- loadings: bfloat16 [20, 4096], P(None, 'bin'), may hold values from -0.09375 to 0.09375
Outputs:
- zscore: bfloat16 [32768, 4096], P(('samp', 'bin'))
- scores: float32 [32768, 20], P(('samp', 'bin'))
All inputs are finite; a program needn't handle non-finite values.
Results may differ from a plain program's by a relative error of at most 0.017.
Values may be sent and summed in bfloat16 or wider, within the bound.
A program may use at most 128 MiB of HBM per device.

v0:
```python
import jax
import jax.numpy as jnp
from jax import lax
from jax.sharding import PartitionSpec as P

RADIUS = 16


def with_halo(block, sides, width):
    for axis, dim in sides:
        count = lax.axis_size(axis)
        forward = [(i, i + 1) for i in range(count - 1)]
        backward = [(target, source) for source, target in forward]
        low = lax.ppermute(
            lax.slice_in_dim(block, block.shape[dim] - width, None, axis=dim), axis, forward
        )
        high = lax.ppermute(lax.slice_in_dim(block, 0, width, axis=dim), axis, backward)
        block = jnp.concatenate([low, block, high], axis=dim)
    return block


def standardize(residual):
    row_mean = jnp.mean(residual, axis=2, keepdims=True)
    shifted = residual - row_mean
    variance = jnp.mean(shifted * shifted, axis=2, keepdims=True)
    return (shifted / jnp.sqrt(variance + 1e-05)).astype(jnp.bfloat16)


def band_matrix(weight_local, kernel, bin_count):
    width = bin_count + 2 * RADIUS
    inner = jnp.arange(width)[:, None]
    outer = jnp.arange(bin_count)[None, :]
    offset = inner - outer
    valid = (offset >= 0) & (offset <= 2 * RADIUS)
    taps = kernel[jnp.clip(offset, 0, 2 * RADIUS)]
    band = jnp.where(valid, taps * weight_local[:, None], jnp.float32(0.0))
    return (band, jnp.sum(band, axis=0))


def band_smooth(padded, band):
    upper = band.astype(jnp.bfloat16)
    lower = (band - upper.astype(jnp.float32)).astype(jnp.bfloat16)
    first = jnp.dot(padded, upper, preferred_element_type=jnp.float32)
    return first + jnp.dot(padded, lower, preferred_element_type=jnp.float32)


def smooth_window(padded, weight_local, kernel, bin_count):
    band, denominator = band_matrix(weight_local, kernel, bin_count)
    smoothed = band_smooth(padded, band) / denominator
    column = jnp.sum(padded.astype(jnp.float32), axis=0)
    column_smooth = jnp.dot(column, band, precision=lax.Precision.HIGHEST) / denominator
    return (smoothed, column_smooth)


def shard_centred(read_depth, weight_padded, kernel):
    row_count, bin_count = read_depth.shape
    bin_index = lax.axis_index("bin")
    padded = with_halo(read_depth, (("bin", 1),), RADIUS)
    weight_local = lax.dynamic_slice_in_dim(
        weight_padded, bin_index * bin_count, bin_count + 2 * RADIUS
    )
    smoothed, column_smooth = smooth_window(padded, weight_local, kernel, bin_count)
    totals = lax.psum(column_smooth, "samp")
    bin_mean = totals / (row_count * lax.axis_size("samp"))
    return (smoothed - bin_mean).astype(jnp.bfloat16)


def on_device(read_depth, gc_weight, map_weight, kernel, loadings):
    row_count, bin_count = read_depth.shape
    bin_devices = lax.axis_size("bin")
    row_share = row_count // bin_devices
    weights = gc_weight * map_weight
    weight_padded = jnp.pad(weights, (RADIUS, RADIUS))
    centred = shard_centred(read_depth, weight_padded, kernel)
    full_loadings = lax.all_gather(loadings, "bin", axis=1, tiled=True)
    sectioned = centred.reshape(bin_devices, row_share, bin_count)
    sample_rows = lax.all_to_all(sectioned, "bin", split_axis=0, concat_axis=2, tiled=True)[0]
    row_scores = jnp.dot(sample_rows, full_loadings.T, preferred_element_type=jnp.float32)
    residual = sample_rows - jnp.dot(
        row_scores, full_loadings.astype(jnp.float32), precision=lax.Precision.HIGHEST
    )
    zscore = standardize(residual[None])
    scores = row_scores[None]
    return (
        zscore.reshape(row_share, bin_count * bin_devices),
        scores.reshape(row_share, scores.shape[2]),
    )


def solution(mesh):
    return jax.shard_map(
        on_device,
        mesh=mesh,
        in_specs=(P("samp", "bin"), P(), P(), P(), P(None, "bin")),
        out_specs=(P(("samp", "bin"), None), P(("samp", "bin"), None)),
        check_vma=False,
    )
```

profile of v0, /device:TPU:0, one launch (start us, length us, event | category | flops | bytes accessed | tf_op | source)
XLA Modules:
  0.0 407.4 jit_solution(13668735623705919041)
XLA Ops:
  0.6 4.3 %fusion.194 = (bf16[8192,16]{1,0:T(8,128)(2,1)}, bf16[8192,16]{1,0:T(8,128)(2,1)S(1)}) fusion(bf16[8192,512]{1,0:T(8,128)(2,1)} %param.5), kind=kLoop, calls=%fused_computation.205 | loop fusion | bytes 1048576 | tf_op jit(solution)/shard_map/slice | solution.py:15
  4.9 1.8 copy.18
  6.7 4.9 %collective-permute-start = (bf16[8192,16]{0,1:T(8,128)(2,1)S(1)}, bf16[8192,16]{0,1:T(8,128)(2,1)S(1)}, u32[]{:S(2)}, u32[]{:S(2)}) collective-permute-start(bf16[8192,16]{0,1:T(8,128)(2,1)S(1)} %copy.18), channel_id=1, source_target_pairs={{0,1},{1,2},{2,3},{3,4},{4,5},{5,6},{6,7},{8,9},{9,10},{10,11},{11... | collective-permute-start | bytes 786440 | tf_op jit(solution)/shard_map/ppermute | solution.py:14
  11.7 0.8 copy.19
  12.4 1.3 collective-permute-start.1
  13.8 0.7 fusion.195
  14.5 0.7 fusion.196
  15.2 0.1 pad_dynamic-slice_fusion
  15.3 23.6 %fusion.84 = f32[512]{0:T(512)S(1)} fusion(f32[544]{0:T(1024)S(1)} %pad_dynamic-slice_fusion, f32[]{:T(128)} %bitcast.58, f32[]{:T(128)} %bitcast.57, f32[]{:T(128)} %bitcast.56, f32[]{:T(128)} %bitcast.55, f32[]{:T(128)} %bitcast.54, f32[]{:T(128)} %bitcast.53, f32[]{:T(128)} %bitcast.52, f32[]{:T(128)} %bitcast.51, f32[]{:T(128)} %bitcast.49, f32[]{:T(128)} %bitcast.47, ...), kind=kLoop, calls=%fused_computation.94 | loop fusion | flops 21167616 | bytes 4356 | tf_op jit(solution)/shard_map/reduce_sum | solution.py:37
  39.0 1.0 copy.15
  40.0 1.8 copy.16
  41.8 37.4 %fusion.81 = f32[8192,512]{1,0:T(8,128)} fusion(f32[]{:T(128)} %bitcast.52, f32[]{:T(128)} %bitcast.53, f32[]{:T(128)} %bitcast.54, f32[]{:T(128)} %bitcast.55, f32[]{:T(128)} %bitcast.56, f32[]{:T(128)} %bitcast.58, f32[]{:T(128)} %bitcast.57, f32[]{:T(128)} %bitcast.1, f32[]{:T(128)} %bitcast.3, f32[]{:T(128)} %bitcast.5, f32[]{:T(128)} %bitcast.7, ...), kind=kOutput, calls=%fused_computation.92 | convolution fusion | flops 4612145152 | bytes 25692420 | tf_op jit(solution)/shard_map/dot_general | solution.py:44
  79.2 8.5 %convert_reduce_fusion = f32[544]{0:T(1024)S(1)} fusion(bf16[8192,16]{1,0:T(8,128)(2,1)S(1)} %copy-done.1, bf16[8192,512]{1,0:T(8,128)(2,1)} %param.5, bf16[8192,16]{1,0:T(8,128)(2,1)S(1)} %copy.15), kind=kLoop, calls=%fused_computation | loop fusion | flops 31194592 | bytes 8915072 | tf_op jit(solution)/shard_map/reduce_sum | solution.py:50
  87.7 21.8 %fusion.82 = f32[1,512]{1,0:T(1,128)S(1)} fusion(f32[544,1]{0,1:T(1,128)S(1)} %reshape.190, f32[]{:T(128)} %bitcast.52, f32[]{:T(128)} %bitcast.53, f32[]{:T(128)} %bitcast.54, f32[]{:T(128)} %bitcast.55, f32[]{:T(128)} %bitcast.56, f32[]{:T(128)} %bitcast.58, f32[]{:T(128)} %bitcast.57, f32[]{:T(128)} %bitcast.1, f32[]{:T(128)} %bitcast.3, f32[]{:T(128)} %bitcast.5, ...), kind=kOutput, calls=%fused_computation.93 | convolution fusion | flops 24231936 | bytes 6532 | tf_op jit(solution)/shard_map/dot_general | solution.py:51
  109.6 6.5 %psum.7 = f32[512]{0:T(512)S(1)} all-reduce(f32[512]{0:T(512)S(1)} %div.34), channel_id=1, replica_groups=mesh['samp'=4,'bin'=8] {'samp'}, use_global_device_ids=true, to_apply=%region_2.3 | all-reduce | flops 512 | bytes 4096 | tf_op jit(solution)/shard_map/psum | solution.py:63
  116.0 38.9 %subtract_convert_fusion = bf16[8192,512]{1,0:T(8,128)(2,1)} fusion(f32[8192,512]{1,0:T(8,128)} %fusion.81, f32[512]{0:T(512)S(1)} %broadcast_multiply_fusion.1, f32[512]{0:T(512)S(1)} %fusion.84, f32[544]{0:T(1024)S(1)} %pad_dynamic-slice_fusion, f32[]{:T(128)} %bitcast.58, f32[]{:T(128)} %bitcast.57, f32[]{:T(128)} %bitcast.56, f32[]{:T(128)} %bitcast.55, ...), kind=kOutput, calls=%fused_computation.4 | convolution fusion | flops 4628086784 | bytes 34085124 | tf_op jit(solution)/shard_map/dot_general | solution.py:43
  154.9 6.8 %all-to-all-start = ((bf16[8,1024,512]{2,1,0:T(8,128)(2,1)}), bf16[8,1024,512]{2,1,0:T(8,128)(2,1)}, u32[]{:S(2)}, u32[]{:S(2)}) async-start(bf16[8,1024,512]{2,1,0:T(8,128)(2,1)} %bitcast.520), calls=%async_computation | async-start | bytes 16777216 | tf_op jit(solution)/shard_map/all_to_all | solution.py:77
  161.7 203.0 %all_gather.3 = bf16[20,4096]{1,0:T(8,128)(2,1)S(1)} all-gather(bf16[20,512]{1,0:T(8,128)(2,1)S(1)} %copy-done.4), channel_id=1, replica_groups=mesh['samp'=4,'bin'=8] {'bin'}, dimensions={1}, use_global_device_ids=true | all-gather | bytes 184320 | tf_op jit(solution)/shard_map/all_gather | solution.py:75
  364.8 8.1 %copy.20 = bf16[128,8,8,512]{3,1,2,0:T(8,128)(2,1)} copy(bf16[128,8,8,512]{3,1,0,2:T(8,128)(2,1)} %bitcast.511) | data formatting | bytes 16777216
  372.8 5.8 %fusion.198 = f32[1024,20]{0,1:T(8,128)S(1)} fusion(bf16[1024,4096]{1,0:T(8,128)(2,1)} %bitcast.518, bf16[20,4096]{1,0:T(8,128)(2,1)S(1)} %all_gather.3), kind=kOutput, calls=%fused_computation.209 | convolution fusion | flops 167772160 | bytes 8634368 | tf_op jit(solution)/shard_map/dot_general | solution.py:78
  378.7 0.0 copy-start.2
  378.7 11.3 %fusion.197 = (f32[1024]{0:T(1024)S(1)}, f32[1024,4096]{1,0:T(8,128)}) fusion(f32[1024,20]{0,1:T(8,128)S(1)} %fusion.198, bf16[20,4096]{1,0:T(8,128)(2,1)S(1)} %all_gather.3, bf16[1024,4096]{1,0:T(8,128)(2,1)S(1)} %bitcast.519), kind=kOutput, calls=%fused_computation.208 | convolution fusion | flops 1019214848 | bytes 25415680 | tf_op jit(solution)/shard_map/dot_general | solution.py:79
  390.0 7.5 %multiply_reduce_fusion = f32[1024]{0:T(1024)S(1)} fusion(f32[1024,4096]{1,0:T(8,128)} %get-tuple-element.38, f32[1024]{0:T(1024)S(1)} %broadcast_multiply_fusion), kind=kLoop, calls=%fused_computation.2 | loop fusion | flops 12581888 | bytes 16785408 | tf_op jit(solution)/shard_map/reduce_sum | solution.py:25
  397.6 9.8 %divide_convert_fusion = bf16[1024,4096]{1,0:T(8,128)(2,1)} fusion(f32[1024,4096]{1,0:T(8,128)} %get-tuple-element.38, f32[1024]{0:T(1024)S(1)} %add_sqrt_fusion, f32[1024]{0:T(1024)S(1)} %broadcast_multiply_fusion), kind=kLoop, calls=%fused_computation.1 | loop fusion | flops 12582912 | bytes 25174016 | tf_op jit(solution)/shard_map/convert_element_type | solution.py:26
  (22 shorter events, 0.1 us)
Async XLA Ops:
  6.7 32.2 %collective-permute-start = (bf16[8192,16]{0,1:T(8,128)(2,1)S(1)}, bf16[8192,16]{0,1:T(8,128)(2,1)S(1)}, u32[]{:S(2)}, u32[]{:S(2)}) collective-permute-start(bf16[8192,16]{0,1:T(8,128)(2,1)S(1)} %copy.18), channel_id=1, source_target_pairs={{0,1},{1,2},{2,3},{3,4},{4,5},{5,6},{6,7},{8,9},{9,10},{10,11},{11... | collective-permute-start | bytes 786440 | tf_op jit(solution)/shard_map/ppermute | solution.py:14
  11.6 2.1 copy-start.3
  11.6 3.6 copy-start.5
  11.7 3.5 copy-start.6
  12.4 27.6 %collective-permute-start.1 = (bf16[8192,16]{0,1:T(8,128)(2,1)S(1)}, bf16[8192,16]{0,1:T(8,128)(2,1)S(1)}, u32[]{:S(2)}, u32[]{:S(2)}) collective-permute-start(bf16[8192,16]{0,1:T(8,128)(2,1)S(1)} %copy.19), channel_id=1, source_target_pairs={{1,0},{2,1},{3,2},{4,3},{5,4},{6,5},{7,6},{9,8},{10,9},{11,10},{12... | collective-permute-start | bytes 786440 | tf_op jit(solution)/shard_map/ppermute | solution.py:17
  41.8 37.4 %copy-start.1 = (bf16[8192,16]{1,0:T(8,128)(2,1)S(1)}, bf16[8192,16]{1,0:T(8,128)(2,1)}, u32[]{:S(2)}) copy-start(bf16[8192,16]{1,0:T(8,128)(2,1)} %copy.16) | copy-start | bytes 786436
  154.9 6.8 %copy-start.4 = (bf16[20,512]{1,0:T(8,128)(2,1)S(1)}, bf16[20,512]{1,0:T(8,128)(2,1)}, u32[]{:S(2)}) copy-start(bf16[20,512]{1,0:T(8,128)(2,1)} %param.9) | copy-start | bytes 61444
  154.9 209.8 %all-to-all-start = ((bf16[8,1024,512]{2,1,0:T(8,128)(2,1)}), bf16[8,1024,512]{2,1,0:T(8,128)(2,1)}, u32[]{:S(2)}, u32[]{:S(2)}) async-start(bf16[8,1024,512]{2,1,0:T(8,128)(2,1)} %bitcast.520), calls=%async_computation | async-start | bytes 16777216 | tf_op jit(solution)/shard_map/all_to_all | solution.py:77
  372.8 5.8 %copy-start = (bf16[128,8,8,512]{3,1,2,0:T(8,128)(2,1)S(1)}, bf16[128,8,8,512]{3,1,2,0:T(8,128)(2,1)}, u32[]{:S(2)}) copy-start(bf16[128,8,8,512]{3,1,2,0:T(8,128)(2,1)} %copy.20) | copy-start | bytes 25165828
  378.7 11.4 %copy-start.2 = (f32[1024,20]{0,1:T(8,128)}, f32[1024,20]{0,1:T(8,128)S(1)}, u32[]{:S(2)}) copy-start(f32[1024,20]{0,1:T(8,128)S(1)} %fusion.198) | copy-start | bytes 245764
where the time goes:
time: 409 us; the launch traced here: 407 us
  blocking collectives  210 us (51%)
  matrix products  115 us (28%)
  other arithmetic  49.5 us (12%)
  local copies, waits for them, and re-layouts  19.3 us (5%)
  starting transfers between devices  13 us (3%)
    all_gather x1, blocking collectives, on_device(): full_loadings = lax.all_gather(loadings, 'bin', axis=1, tiled=True)  203 us
    dot_general x1, matrix products, band_smooth(): first = jnp.dot(padded, upper, preferred_element_type=jnp.float32)  38.9 us
    dot_general x1, matrix products, band_smooth(): return first + jnp.dot(padded, lower, preferred_element_type=jnp.float32)  37.4 us
    reduce_sum x1, other arithmetic, band_matrix(): return (band, jnp.sum(band, axis=0))  23.6 us
    dot_general x1, matrix products, smooth_window(): jnp.dot(column, band, precision=lax.Precision.HIGHEST) / denominator  21.8 us
    dot_general x1, matrix products, on_device(): jnp.dot(row_scores, full_loadings.astype(jnp.float32), precision=lax.Prec...  11.3 us
    unnamed x17, local copies, waits for them, and re-layouts  10.7 us
    convert_element_type x1, other arithmetic, standardize(): return (shifted / jnp.sqrt(variance + 1e-05)).astype(jnp.bfloat16)  9.81 us
  transfers between devices with their start and end apart: 3, of which 0 were waited for; matrix products, arithmetic and copies ran while one was open for 7% of the time, Pallas kernels for 0%

commit v1 on v0

v1 whole, which is shorter than its diff:
```python
import functools

import jax
import jax.numpy as jnp
from jax import lax
from jax.experimental import pallas as pl
from jax.experimental.pallas import tpu as pltpu
from jax.sharding import PartitionSpec as P

RADIUS = 16
EDGE = 128
OUT = 256
WIN = OUT + 2 * EDGE
CHUNK = 128
AHEAD = 3
EPS = 1e-05
MESH = pl.DeviceIdType.MESH
F32 = jnp.float32
BF16 = jnp.bfloat16


def peer_order(count):
    return sorted(range(1, count), key=lambda step: (abs(2 * step - count), step))


def split3(value):
    first = value.astype(BF16)
    rest = value - first.astype(F32)
    second = rest.astype(BF16)
    third = (rest - second.astype(F32)).astype(BF16)
    return first, second, third


def kernel(
    n_samp, n_bin, x_ref, gc_ref, map_ref, taps_ref, load_ref, z_ref, scores_ref,
    land, xbuf, toeplitz, band, wpad, mrows, mean, part, parts, total, totals,
    lpad, lall, lstack, cent, resid, zbuf,
    local_sem, x_sem, out_sem, send_sem, recv_sem, lsend, lrecv, psend, precv, tsend, trecv,
):
    rows, width = x_ref.shape
    share = rows // n_bin
    bins = width * n_bin
    chunks = share // CHUNK
    blocks = bins // OUT
    comps = load_ref.shape[0]
    kpad = lpad.shape[0]
    samp, me = lax.axis_index("samp"), lax.axis_index("bin")
    order = peer_order(n_bin)
    pieces = x_sem.shape[0]
    piece = rows // pieces

    def columns(index):
        return pl.ds(pl.multiple_of(index * width, width), width)

    def landed(index):
        return pl.ds(pl.multiple_of(EDGE + index * width, EDGE), width)

    own = pltpu.make_async_copy(
        x_ref.at[pl.ds(pl.multiple_of(me * share, share), share), :],
        land.at[:, landed(me)], local_sem,
    )
    loads = [
        pltpu.make_async_copy(
            x_ref.at[pl.ds(p * piece, piece), :], xbuf.at[pl.ds(p * piece, piece), :], x_sem.at[p]
        )
        for p in range(pieces)
    ]
    for copy in loads:
        copy.start()
    own.start()

    barrier = pltpu.get_barrier_semaphore()
    for step in range(1, n_bin):
        pl.semaphore_signal(
            barrier, inc=1, device_id={"bin": lax.rem(me + step, n_bin)}, device_id_type=MESH
        )
    for step in range(1, n_samp):
        pl.semaphore_signal(
            barrier, inc=1, device_id={"samp": lax.rem(samp + step, n_samp)}, device_id_type=MESH
        )
    lpad[...] = jnp.zeros(lpad.shape, BF16)
    lpad[pl.ds(0, comps), :] = load_ref[...]
    pl.semaphore_wait(barrier, n_bin + n_samp - 2)

    def load_copy(step, owner):
        return pltpu.make_async_remote_copy(
            src_ref=lpad, dst_ref=lall.at[:, columns(owner)],
            send_sem=lsend.at[step - 1], recv_sem=lrecv.at[step - 1],
            device_id={"bin": lax.rem(me + step, n_bin)}, device_id_type=MESH,
        )

    def block_copy(chunk, step, owner):
        to = lax.rem(me + step, n_bin)
        start = pl.multiple_of(to * share + chunk * CHUNK, CHUNK)
        return pltpu.make_async_remote_copy(
            src_ref=x_ref.at[pl.ds(start, CHUNK), :],
            dst_ref=land.at[pl.ds(pl.multiple_of(chunk * CHUNK, CHUNK), CHUNK), landed(owner)],
            send_sem=send_sem.at[chunk, step - 1], recv_sem=recv_sem.at[chunk, step - 1],
            device_id={"bin": to}, device_id_type=MESH,
        )

    def part_copy(step, owner):
        return pltpu.make_async_remote_copy(
            src_ref=part, dst_ref=parts.at[owner],
            send_sem=psend.at[step - 1], recv_sem=precv.at[step - 1],
            device_id={"samp": lax.rem(samp + step, n_samp)}, device_id_type=MESH,
        )

    def total_copy(step, owner):
        return pltpu.make_async_remote_copy(
            src_ref=total, dst_ref=totals.at[:, columns(owner)],
            send_sem=tsend.at[step - 1], recv_sem=trecv.at[step - 1],
            device_id={"bin": lax.rem(me + step, n_bin)}, device_id_type=MESH,
        )

    def bin_source(step):
        return lax.rem(me + n_bin - step, n_bin)

    def send_chunk(chunk):
        for step in order:
            block_copy(chunk, step, me).start()

    for step in order:
        load_copy(step, me).start()
    first = min(2, chunks)
    for chunk in range(first):
        send_chunk(chunk)

    part[...] = jnp.zeros(part.shape, F32)
    group = 128
    for p in range(pieces):
        loads[p].wait()

        def add_rows(i, carry, p=p):
            start = pl.multiple_of(p * piece + i * group, group)
            block = xbuf[pl.ds(start, group), :].astype(F32)
            part[...] += jnp.sum(block.reshape(group // 8, 8, width), axis=0)
            return carry

        lax.fori_loop(0, piece // group, add_rows, 0)
    for step in range(1, n_samp):
        part_copy(step, samp).start()
    parts[samp] = part[...]

    wpad[...] = jnp.zeros(wpad.shape, F32)
    wpad[pl.ds(0, 1), pl.ds(EDGE, bins)] = gc_ref[...] * map_ref[...]
    toeplitz[...] = jnp.zeros(toeplitz.shape, F32)
    offset = (
        lax.broadcasted_iota(jnp.int32, (WIN, OUT), 0)
        - lax.broadcasted_iota(jnp.int32, (WIN, OUT), 1)
        - (EDGE - RADIUS)
    )

    def add_tap(tap, carry):
        toeplitz[...] = jnp.where(offset == tap, taps_ref[tap], toeplitz[...])
        return carry

    lax.fori_loop(0, 2 * RADIUS + 1, add_tap, 0)

    def make_band(j, carry):
        weight = wpad[pl.ds(0, 1), pl.ds(pl.multiple_of(j * OUT, OUT), WIN)]
        tall = jnp.transpose(jnp.broadcast_to(weight, (128, WIN)))
        raw = jnp.concatenate([tall] * (OUT // 128), axis=1) * toeplitz[...]
        scaled = raw * (1.0 / jnp.sum(raw, axis=0, keepdims=True))
        upper = scaled.astype(BF16)
        band[j, pl.ds(0, WIN), :] = upper
        band[j, pl.ds(WIN, WIN), :] = (scaled - upper.astype(F32)).astype(BF16)
        return carry

    for step in range(1, n_samp):
        copy = part_copy(step, lax.rem(samp + n_samp - step, n_samp))
        copy.wait_recv()
    summed = parts[0]
    for s in range(1, n_samp):
        summed = summed + parts[s]
    total[...] = jnp.broadcast_to(jnp.sum(summed, axis=0, keepdims=True), total.shape)
    for step in order:
        total_copy(step, me).start()
    totals[:, columns(me)] = total[...]
    for chunk in range(first, min(AHEAD, chunks)):
        send_chunk(chunk)

    lax.fori_loop(0, blocks, make_band, 0)

    land[:, pl.ds(0, EDGE)] = jnp.zeros((share, EDGE), BF16)
    land[:, pl.ds(EDGE + bins, EDGE)] = jnp.zeros((share, EDGE), BF16)
    mrows[...] = jnp.zeros(mrows.shape, BF16)

    for step in order:
        load_copy(step, bin_source(step)).wait_recv()
    lall[:, columns(me)] = lpad[...]
    for copy in range(3):
        lstack[pl.ds(copy * kpad, kpad), :] = lall[...]

    for step in order:
        total_copy(step, bin_source(step)).wait_recv()
    mean_raw = totals[pl.ds(0, 1), :] / (rows * n_samp)
    for row, value in enumerate(split3(mean_raw)):
        mrows[pl.ds(row, 1), pl.ds(EDGE, bins)] = value

    def smooth(lhs, j):
        return jnp.dot(
            jnp.concatenate([lhs, lhs], axis=1), band[j], preferred_element_type=F32
        )

    def mean_block(j, carry):
        start = pl.multiple_of(j * OUT, OUT)
        value = smooth(mrows[:, pl.ds(start, WIN)], j)
        mean[:, pl.ds(start, OUT)] = jnp.broadcast_to(
            jnp.sum(value, axis=0, keepdims=True), (8, OUT)
        )
        return carry

    lax.fori_loop(0, blocks, mean_block, 0)
    own.wait()

    def lanes(value):
        folded = value[:, 0:128]
        for k in range(1, OUT // 128):
            folded = folded + value[:, k * 128:(k + 1) * 128]
        return folded

    def out_copy(chunk, slot):
        return pltpu.make_async_copy(
            zbuf.at[slot], z_ref.at[pl.ds(pl.multiple_of(chunk * CHUNK, CHUNK), CHUNK), :],
            out_sem.at[slot],
        )

    def finish(chunk, carry):
        base = pl.multiple_of(chunk * CHUNK, CHUNK)
        slot = lax.rem(chunk, 2)
        for step in order:
            block_copy(chunk, step, bin_source(step)).wait_recv()

        @pl.when(chunk + AHEAD < chunks)
        def _():
            send_chunk(chunk + AHEAD)

        def smooth_block(j, carry):
            start = pl.multiple_of(j * OUT, OUT)
            value = smooth(land[pl.ds(base, CHUNK), pl.ds(start, WIN)], j)
            cent[:, pl.ds(start, OUT)] = (
                value - mean[pl.ds(0, 1), pl.ds(start, OUT)]
            ).astype(BF16)
            return carry

        lax.fori_loop(0, blocks, smooth_block, 0, unroll=2)
        score = lax.dot_general(
            cent[...], lall[...], (((1,), (1,)), ((), ())), preferred_element_type=F32
        )
        scores_ref[pl.ds(base, CHUNK), :] = score[:, 0:comps]
        pieces3 = jnp.concatenate(split3(score), axis=1)

        def residual_block(j, acc):
            cols = pl.ds(pl.multiple_of(j * OUT, OUT), OUT)
            value = cent[:, cols].astype(F32) - jnp.dot(
                pieces3, lstack[:, cols], preferred_element_type=F32
            )
            resid[:, cols] = value
            return acc + lanes(value)

        zero = jnp.zeros((CHUNK, 128), F32)
        acc = lax.fori_loop(0, blocks, residual_block, zero, unroll=2)
        row_mean = jnp.sum(acc, axis=1, keepdims=True) / bins

        def square_block(j, acc):
            cols = pl.ds(pl.multiple_of(j * OUT, OUT), OUT)
            shifted = resid[:, cols] - row_mean
            return acc + lanes(shifted * shifted)

        acc = lax.fori_loop(0, blocks, square_block, zero, unroll=2)
        scale = 1.0 / jnp.sqrt(jnp.sum(acc, axis=1, keepdims=True) / bins + EPS)

        @pl.when(chunk >= 2)
        def _():
            out_copy(chunk - 2, slot).wait()

        def store_block(j, carry):
            cols = pl.ds(pl.multiple_of(j * OUT, OUT), OUT)
            zbuf[slot, :, cols] = ((resid[:, cols] - row_mean) * scale).astype(BF16)
            return carry

        lax.fori_loop(0, blocks, store_block, 0, unroll=2)
        out_copy(chunk, slot).start()
        return carry

    lax.fori_loop(0, chunks, finish, 0)

    def drain(chunk, carry):
        for step in order:
            block_copy(chunk, step, me).wait_send()
        return carry

    lax.fori_loop(0, chunks, drain, 0)
    for step in order:
        load_copy(step, me).wait_send()
        total_copy(step, me).wait_send()
    for step in range(1, n_samp):
        part_copy(step, samp).wait_send()
    for chunk in range(max(0, chunks - 2), chunks):
        out_copy(chunk, chunk % 2).wait()


def on_device(n_samp, n_bin, read_depth, gc_weight, map_weight, taps, loadings):
    rows, width = read_depth.shape
    comps = loadings.shape[0]
    share, bins = rows // n_bin, width * n_bin
    chunks, blocks = share // CHUNK, bins // OUT
    kpad = -(-comps // 32) * 32
    padded = bins + 2 * EDGE
    dma = pltpu.SemaphoreType.DMA
    vmem = pl.BlockSpec(memory_space=pltpu.VMEM)
    anywhere = pl.BlockSpec(memory_space=pl.ANY)
    return pl.pallas_call(
        functools.partial(kernel, n_samp, n_bin),
        out_shape=(
            jax.ShapeDtypeStruct((share, bins), BF16),
            jax.ShapeDtypeStruct((share, comps), F32),
        ),
        in_specs=[anywhere, vmem, vmem, pl.BlockSpec(memory_space=pltpu.SMEM), vmem],
        out_specs=(anywhere, vmem),
        scratch_shapes=[
            pltpu.VMEM((share, padded), BF16),
            pltpu.VMEM((rows, width), BF16),
            pltpu.VMEM((WIN, OUT), F32),
            pltpu.VMEM((blocks, 2 * WIN, OUT), BF16),
            pltpu.VMEM((8, padded), F32),
            pltpu.VMEM((16, padded), BF16),
            pltpu.VMEM((8, bins), F32),
            pltpu.VMEM((8, width), F32),
            pltpu.VMEM((n_samp, 8, width), F32),
            pltpu.VMEM((8, width), F32),
            pltpu.VMEM((8, bins), F32),
            pltpu.VMEM((kpad, width), BF16),
            pltpu.VMEM((kpad, bins), BF16),
            pltpu.VMEM((3 * kpad, bins), BF16),
            pltpu.VMEM((CHUNK, bins), BF16),
            pltpu.VMEM((CHUNK, bins), F32),
            pltpu.VMEM((2, CHUNK, bins), BF16),
            dma,
            dma((4,)),
            dma((2,)),
            dma((chunks, n_bin - 1)),
            dma((chunks, n_bin - 1)),
            dma((n_bin - 1,)),
            dma((n_bin - 1,)),
            dma((n_samp - 1,)),
            dma((n_samp - 1,)),
            dma((n_bin - 1,)),
            dma((n_bin - 1,)),
        ],
        compiler_params=pltpu.CompilerParams(
            collective_id=0, has_side_effects=True, vmem_limit_bytes=56 * 1024 * 1024
        ),
        name="denoise",
    )(
        read_depth, gc_weight.reshape(1, bins), map_weight.reshape(1, bins), taps, loadings
    )


def solution(mesh):
    return jax.shard_map(
        functools.partial(on_device, mesh.shape["samp"], mesh.shape["bin"]),
        mesh=mesh,
        in_specs=(P("samp", "bin"), P(), P(), P(), P(None, "bin")),
        out_specs=(P(("samp", "bin"), None), P(("samp", "bin"), None)),
        check_vma=False,
    )
```

time: 409 us -> 213 us (0.52)
  blocking collectives: 210 us -> 0 us
  Pallas kernels: 0 us -> 200 us
  matrix products: 115 us -> 0 us
  other arithmetic: 49.5 us -> 0 us
  starting transfers between devices: 13 us -> 0 us
  local copies, waits for them, and re-layouts: 19.3 us -> 9.76 us
    all_gather x1 -> x0, blocking collectives: 203 us -> none  [on_device(): full_loadings = lax.all_gather(loadings, 'bin', axis=1, tiled=True)]
    pallas_call x0 -> x1, Pallas kernels: none -> 200 us  [on_device(): pl.pallas_call(functools.partial(kernel, n_samp, n_bin), out_shape=(jax.S...]
    dot_general x5 -> x0, matrix products: 115 us -> none  [the longest x1 38.9 us: band_smooth(): first = jnp.dot(padded, upper, preferred_element_type=jnp.float32)]
    reduce_sum x3 -> x0, other arithmetic: 39.7 us -> none  [the longest x1 23.6 us: band_matrix(): return (band, jnp.sum(band, axis=0))]
    convert_element_type x1 -> x0, other arithmetic: 9.81 us -> none  [standardize(): return (shifted / jnp.sqrt(variance + 1e-05)).astype(jnp.bfloat16)]
    all_to_all x1 -> x0, starting transfers between devices: 6.81 us -> none  [on_device(): lax.all_to_all(sectioned, 'bin', split_axis=0, concat_axis=2, tiled=True)[0]]
    psum x1 -> x0, blocking collectives: 6.48 us -> none  [shard_centred(): totals = lax.psum(column_smooth, 'samp')]
    ppermute x2 -> x0, starting transfers between devices: 6.18 us -> none  [the longest x1 4.89 us: with_halo(): lax.ppermute(lax.slice_in_dim(block, block.shape[dim] - width, None, axis...]
  transfers between devices with their start and end apart: 3 -> 0, of which waited for: 0 -> 0; matrix products, arithmetic and copies ran while one was open for 7% -> 0% of each run, Pallas kernels for 0% -> 0%
where the time goes in v1:
time: 213 us; the launch traced here: 211 us
  Pallas kernels  200 us (94%)
  local copies, waits for them, and re-layouts  9.76 us (5%)
    pallas_call x1, Pallas kernels, on_device(): pl.pallas_call(functools.partial(kernel, n_samp, n_bin), out_shape=(jax.S...  200 us
    unnamed x1, local copies, waits for them, and re-layouts  7.89 us

profile of v1, /device:TPU:0, one launch (start us, length us, event | category | flops | bytes accessed | tf_op | source)
XLA Modules:
  0.0 210.8 jit_solution(11693186382857230856)
XLA Ops:
  0.6 200.4 %denoise.1 = (bf16[1024,4096]{1,0:T(8,128)(2,1)}, f32[1024,20]{1,0:T(8,128)}) custom-call(bf16[8192,512]{1,0:T(8,128)(2,1)} %x_ref.1, f32[1,4096]{1,0:T(1,128)} %bitcast.2, f32[1,4096]{1,0:T(1,128)} %bitcast.3, f32[33]{0:T(128)} %taps_ref.1, bf16[20,512]{1,0:T(8,128)(2,1)} %load_ref.1), custom_call_target="tpu_custom_call" | custom-call | tf_op jit(solution)/shard_map/denoise/pallas_call | solution.py:314
  201.0 1.9 copy.7
  202.9 7.9 %copy.9 = bf16[1024,4096]{1,0:T(8,128)(2,1)} copy(bf16[1024,4096]{1,0:T(8,128)(2,1)} %get-tuple-element.6) | data formatting | bytes 16777216

commit v2 on v1

--- a/solution.py
+++ b/solution.py
@@ -34,8 +34,8 @@
 def kernel(
     n_samp, n_bin, x_ref, gc_ref, map_ref, taps_ref, load_ref, z_ref, scores_ref,
     land, xbuf, toeplitz, band, wpad, mrows, mean, part, parts, total, totals,
-    lpad, lall, lstack, cent, resid, zbuf,
-    local_sem, x_sem, out_sem, send_sem, recv_sem, lsend, lrecv, psend, precv, tsend, trecv,
+    lpad, lparts, lall, lstack, cent, resid, zbuf,
+    local_sem, x_sem, out_sem, send_sem, recv_sem, lsend, lrecv, ssend, srecv, psend, precv, tsend, trecv,
 ):
     rows, width = x_ref.shape
     share = rows // n_bin
@@ -44,6 +44,8 @@
     blocks = bins // OUT
     comps = load_ref.shape[0]
     kpad = lpad.shape[0]
+    lgroups = lparts.shape[0]
+    lwidth = width // lgroups
     samp, me = lax.axis_index("samp"), lax.axis_index("bin")
     order = peer_order(n_bin)
     pieces = x_sem.shape[0]
@@ -59,13 +61,14 @@
         x_ref.at[pl.ds(pl.multiple_of(me * share, share), share), :],
         land.at[:, landed(me)], local_sem,
     )
+    slots = xbuf.shape[0]
     loads = [
         pltpu.make_async_copy(
-            x_ref.at[pl.ds(p * piece, piece), :], xbuf.at[pl.ds(p * piece, piece), :], x_sem.at[p]
+            x_ref.at[pl.ds(p * piece, piece), :], xbuf.at[p % slots], x_sem.at[p]
         )
         for p in range(pieces)
     ]
-    for copy in loads:
+    for copy in loads[:slots]:
         copy.start()
     own.start()
 
@@ -80,13 +83,28 @@
         )
     lpad[...] = jnp.zeros(lpad.shape, BF16)
     lpad[pl.ds(0, comps), :] = load_ref[...]
+
+    @pl.when(samp < lgroups)
+    def _():
+        lparts[samp, :, pl.ds(pl.multiple_of(me * lwidth, lwidth), lwidth)] = lpad[
+            :, pl.ds(pl.multiple_of(samp * lwidth, lwidth), lwidth)
+        ]
+
     pl.semaphore_wait(barrier, n_bin + n_samp - 2)
 
     def load_copy(step, owner):
         return pltpu.make_async_remote_copy(
-            src_ref=lpad, dst_ref=lall.at[:, columns(owner)],
+            src_ref=lpad.at[:, pl.ds(pl.multiple_of(samp * lwidth, lwidth), lwidth)],
+            dst_ref=lparts.at[samp, :, pl.ds(pl.multiple_of(owner * lwidth, lwidth), lwidth)],
             send_sem=lsend.at[step - 1], recv_sem=lrecv.at[step - 1],
             device_id={"bin": lax.rem(me + step, n_bin)}, device_id_type=MESH,
+        )
+
+    def spread_copy(step, owner):
+        return pltpu.make_async_remote_copy(
+            src_ref=lparts.at[owner], dst_ref=lparts.at[owner],
+            send_sem=ssend.at[step - 1], recv_sem=srecv.at[step - 1],
+            device_id={"samp": lax.rem(samp + step, n_samp)}, device_id_type=MESH,
         )
 
     def block_copy(chunk, step, owner):
@@ -120,8 +138,11 @@
         for step in order:
             block_copy(chunk, step, me).start()
 
-    for step in order:
-        load_copy(step, me).start()
+    @pl.when(samp < lgroups)
+    def _():
+        for step in order:
+            load_copy(step, me).start()
+
     first = min(2, chunks)
     for chunk in range(first):
         send_chunk(chunk)
@@ -132,12 +153,14 @@
         loads[p].wait()
 
         def add_rows(i, carry, p=p):
-            start = pl.multiple_of(p * piece + i * group, group)
-            block = xbuf[pl.ds(start, group), :].astype(F32)
+            start = pl.multiple_of(i * group, group)
+            block = xbuf[p % slots, pl.ds(start, group), :].astype(F32)
             part[...] += jnp.sum(block.reshape(group // 8, 8, width), axis=0)
             return carry
 
         lax.fori_loop(0, piece // group, add_rows, 0)
+        if p + slots < pieces:
+            loads[p + slots].start()
     for step in range(1, n_samp):
         part_copy(step, samp).start()
     parts[samp] = part[...]
@@ -173,28 +196,44 @@
     summed = parts[0]
     for s in range(1, n_samp):
         summed = summed + parts[s]
-    total[...] = jnp.broadcast_to(jnp.sum(summed, axis=0, keepdims=True), total.shape)
+    total[...] = jnp.sum(summed, axis=0, keepdims=True)
     for step in order:
         total_copy(step, me).start()
     totals[:, columns(me)] = total[...]
     for chunk in range(first, min(AHEAD, chunks)):
         send_chunk(chunk)
 
+    @pl.when(samp < lgroups)
+    def _():
+        for step in order:
+            load_copy(step, bin_source(step)).wait_recv()
+        for step in range(1, n_samp):
+            spread_copy(step, samp).start()
+
     lax.fori_loop(0, blocks, make_band, 0)
 
     land[:, pl.ds(0, EDGE)] = jnp.zeros((share, EDGE), BF16)
     land[:, pl.ds(EDGE + bins, EDGE)] = jnp.zeros((share, EDGE), BF16)
     mrows[...] = jnp.zeros(mrows.shape, BF16)
 
-    for step in order:
-        load_copy(step, bin_source(step)).wait_recv()
-    lall[:, columns(me)] = lpad[...]
+    for step in range(1, n_samp):
+        owner = lax.rem(samp + n_samp - step, n_samp)
+
+        @pl.when(owner < lgroups)
+        def _(step=step, owner=owner):
+            spread_copy(step, owner).wait_recv()
+
+    for b in range(n_bin):
+        for g in range(lgroups):
+            lall[:, pl.ds(b * width + g * lwidth, lwidth)] = lparts[
+                g, :, pl.ds(b * lwidth, lwidth)
+            ]
     for copy in range(3):
         lstack[pl.ds(copy * kpad, kpad), :] = lall[...]
 
     for step in order:
         total_copy(step, bin_source(step)).wait_recv()
-    mean_raw = totals[pl.ds(0, 1), :] / (rows * n_samp)
+    mean_raw = totals[...] / (rows * n_samp)
     for row, value in enumerate(split3(mean_raw)):
         mrows[pl.ds(row, 1), pl.ds(EDGE, bins)] = value
 
@@ -248,7 +287,7 @@
         score = lax.dot_general(
             cent[...], lall[...], (((1,), (1,)), ((), ())), preferred_element_type=F32
         )
-        scores_ref[pl.ds(base, CHUNK), :] = score[:, 0:comps]
+        scores_ref[:, pl.ds(base, CHUNK)] = jnp.transpose(score)[0:comps, :]
         pieces3 = jnp.concatenate(split3(score), axis=1)
 
         def residual_block(j, acc):
@@ -293,8 +332,15 @@
 
     lax.fori_loop(0, chunks, drain, 0)
     for step in order:
-        load_copy(step, me).wait_send()
         total_copy(step, me).wait_send()
+
+    @pl.when(samp < lgroups)
+    def _():
+        for step in order:
+            load_copy(step, me).wait_send()
+        for step in range(1, n_samp):
+            spread_copy(step, samp).wait_send()
+
     for step in range(1, n_samp):
         part_copy(step, samp).wait_send()
     for chunk in range(max(0, chunks - 2), chunks):
@@ -306,22 +352,23 @@
     comps = loadings.shape[0]
     share, bins = rows // n_bin, width * n_bin
     chunks, blocks = share // CHUNK, bins // OUT
+    lgroups = min(n_samp, width // 128)
     kpad = -(-comps // 32) * 32
     padded = bins + 2 * EDGE
     dma = pltpu.SemaphoreType.DMA
     vmem = pl.BlockSpec(memory_space=pltpu.VMEM)
     anywhere = pl.BlockSpec(memory_space=pl.ANY)
-    return pl.pallas_call(
+    zscore, scores = pl.pallas_call(
         functools.partial(kernel, n_samp, n_bin),
         out_shape=(
             jax.ShapeDtypeStruct((share, bins), BF16),
-            jax.ShapeDtypeStruct((share, comps), F32),
+            jax.ShapeDtypeStruct((comps, share), F32),
         ),
         in_specs=[anywhere, vmem, vmem, pl.BlockSpec(memory_space=pltpu.SMEM), vmem],
         out_specs=(anywhere, vmem),
         scratch_shapes=[
             pltpu.VMEM((share, padded), BF16),
-            pltpu.VMEM((rows, width), BF16),
+            pltpu.VMEM((2, rows // 8, width), BF16),
             pltpu.VMEM((WIN, OUT), F32),
             pltpu.VMEM((blocks, 2 * WIN, OUT), BF16),
             pltpu.VMEM((8, padded), F32),
@@ -329,16 +376,17 @@
             pltpu.VMEM((8, bins), F32),
             pltpu.VMEM((8, width), F32),
             pltpu.VMEM((n_samp, 8, width), F32),
-            pltpu.VMEM((8, width), F32),
-            pltpu.VMEM((8, bins), F32),
+            pltpu.VMEM((1, width), F32),
+            pltpu.VMEM((1, bins), F32),
             pltpu.VMEM((kpad, width), BF16),
+            pltpu.VMEM((lgroups, kpad, width * n_bin // lgroups), BF16),
             pltpu.VMEM((kpad, bins), BF16),
             pltpu.VMEM((3 * kpad, bins), BF16),
             pltpu.VMEM((CHUNK, bins), BF16),
             pltpu.VMEM((CHUNK, bins), F32),
             pltpu.VMEM((2, CHUNK, bins), BF16),
             dma,
-            dma((4,)),
+            dma((8,)),
             dma((2,)),
             dma((chunks, n_bin - 1)),
             dma((chunks, n_bin - 1)),
@@ -346,16 +394,19 @@
             dma((n_bin - 1,)),
             dma((n_samp - 1,)),
             dma((n_samp - 1,)),
+            dma((n_samp - 1,)),
+            dma((n_samp - 1,)),
             dma((n_bin - 1,)),
             dma((n_bin - 1,)),
         ],
         compiler_params=pltpu.CompilerParams(
-            collective_id=0, has_side_effects=True, vmem_limit_bytes=56 * 1024 * 1024
+            collective_id=0, has_side_effects=True, vmem_limit_bytes=48 * 1024 * 1024
         ),
         name="denoise",
     )(
         read_depth, gc_weight.reshape(1, bins), map_weight.reshape(1, bins), taps, loadings
     )
+    return zscore, scores.T
 
 
 def solution(mesh):

time: 213 us -> 207 us (0.972)
  Pallas kernels: 200 us -> 193 us
    pallas_call x1, Pallas kernels: 200 us -> 193 us  [on_device(): pl.pallas_call(functools.partial(kernel, n_samp, n_bin), out_shape=(jax.S...]
    unnamed x1 -> x10, local copies, waits for them, and re-layouts: 7.89 us -> 11.3 us
where the time goes in v2:
time: 207 us; the launch traced here: 205 us
  Pallas kernels  193 us (93%)
  local copies, waits for them, and re-layouts  11.3 us (5%)
    pallas_call x1, Pallas kernels, on_device(): pl.pallas_call(functools.partial(kernel, n_samp, n_bin), out_shape=(jax.S...  193 us
    unnamed x10, local copies, waits for them, and re-layouts  11.3 us

profile of v2, /device:TPU:0, one launch (start us, length us, event | category | flops | bytes accessed | tf_op | source)
XLA Modules:
  0.0 204.6 jit_solution(8638083537928530786)
XLA Ops:
  0.6 0.0 copy-start
  0.6 0.7 copy-done
  1.4 0.0 copy-start.1
  1.4 0.7 copy-done.1
  2.1 0.0 copy-start.2
  2.1 0.7 copy-done.2
  2.8 0.0 copy-start.3
  2.8 0.7 copy-done.3
  3.5 192.6 %denoise.1 = (bf16[1024,4096]{1,0:T(8,128)(2,1)}, f32[20,1024]{1,0:T(8,128)S(1)}) custom-call(bf16[8192,512]{1,0:T(8,128)(2,1)} %x_ref.1, f32[1,4096]{1,0:T(1,128)S(1)} %bitcast.4, f32[1,4096]{1,0:T(1,128)S(1)} %bitcast.5, f32[33]{0:T(128)S(1)} %copy-done.3, bf16[20,512]{1,0:T(8,128)(2,1)S(1)} %copy-done), custom_call_target="tpu_custom_call" | custom-call | tf_op jit(solution)/shard_map/denoise/pallas_call | solution.py:361
  196.1 7.9 %copy.9 = bf16[1024,4096]{1,0:T(8,128)(2,1)} copy(bf16[1024,4096]{1,0:T(8,128)(2,1)} %get-tuple-element.8) | data formatting | bytes 16777216
  204.0 0.6 copy.10
Async XLA Ops:
  0.6 0.7 copy-start
  1.4 0.7 copy-start.1
  2.1 0.7 copy-start.2
  2.8 0.7 copy-start.3

commit v3 on v2

--- a/solution.py
+++ b/solution.py
@@ -34,8 +34,8 @@
 def kernel(
     n_samp, n_bin, x_ref, gc_ref, map_ref, taps_ref, load_ref, z_ref, scores_ref,
     land, xbuf, toeplitz, band, wpad, mrows, mean, part, parts, total, totals,
-    lpad, lparts, lall, lstack, cent, resid, zbuf,
-    local_sem, x_sem, out_sem, send_sem, recv_sem, lsend, lrecv, ssend, srecv, psend, precv, tsend, trecv,
+    lpad, lparts, lall, lstack, cent, resid,
+    local_sem, x_sem, send_sem, recv_sem, lsend, lrecv, ssend, srecv, psend, precv, tsend, trecv,
 ):
     rows, width = x_ref.shape
     share = rows // n_bin
@@ -259,15 +259,8 @@
             folded = folded + value[:, k * 128:(k + 1) * 128]
         return folded
 
-    def out_copy(chunk, slot):
-        return pltpu.make_async_copy(
-            zbuf.at[slot], z_ref.at[pl.ds(pl.multiple_of(chunk * CHUNK, CHUNK), CHUNK), :],
-            out_sem.at[slot],
-        )
-
     def finish(chunk, carry):
         base = pl.multiple_of(chunk * CHUNK, CHUNK)
-        slot = lax.rem(chunk, 2)
         for step in order:
             block_copy(chunk, step, bin_source(step)).wait_recv()
 
@@ -310,17 +303,12 @@
         acc = lax.fori_loop(0, blocks, square_block, zero, unroll=2)
         scale = 1.0 / jnp.sqrt(jnp.sum(acc, axis=1, keepdims=True) / bins + EPS)
 
-        @pl.when(chunk >= 2)
-        def _():
-            out_copy(chunk - 2, slot).wait()
-
         def store_block(j, carry):
             cols = pl.ds(pl.multiple_of(j * OUT, OUT), OUT)
-            zbuf[slot, :, cols] = ((resid[:, cols] - row_mean) * scale).astype(BF16)
+            z_ref[pl.ds(base, CHUNK), cols] = ((resid[:, cols] - row_mean) * scale).astype(BF16)
             return carry
 
         lax.fori_loop(0, blocks, store_block, 0, unroll=2)
-        out_copy(chunk, slot).start()
         return carry
 
     lax.fori_loop(0, chunks, finish, 0)
@@ -343,8 +331,6 @@
 
     for step in range(1, n_samp):
         part_copy(step, samp).wait_send()
-    for chunk in range(max(0, chunks - 2), chunks):
-        out_copy(chunk, chunk % 2).wait()
 
 
 def on_device(n_samp, n_bin, read_depth, gc_weight, map_weight, taps, loadings):
@@ -361,11 +347,11 @@
     zscore, scores = pl.pallas_call(
         functools.partial(kernel, n_samp, n_bin),
         out_shape=(
-            jax.ShapeDtypeStruct((share, bins), BF16),
-            jax.ShapeDtypeStruct((comps, share), F32),
+            pltpu.VMEM((share, bins), BF16),
+            pltpu.VMEM((comps, share), F32),
         ),
         in_specs=[anywhere, vmem, vmem, pl.BlockSpec(memory_space=pltpu.SMEM), vmem],
-        out_specs=(anywhere, vmem),
+        out_specs=(vmem, vmem),
         scratch_shapes=[
             pltpu.VMEM((share, padded), BF16),
             pltpu.VMEM((2, rows // 8, width), BF16),
@@ -384,10 +370,8 @@
             pltpu.VMEM((3 * kpad, bins), BF16),
             pltpu.VMEM((CHUNK, bins), BF16),
             pltpu.VMEM((CHUNK, bins), F32),
-            pltpu.VMEM((2, CHUNK, bins), BF16),
             dma,
             dma((8,)),
-            dma((2,)),
             dma((chunks, n_bin - 1)),
             dma((chunks, n_bin - 1)),
             dma((n_bin - 1,)),

time: 207 us -> 199 us (0.961)
  local copies, waits for them, and re-layouts: 11.3 us -> 4.04 us
    unnamed x10 -> x2, local copies, waits for them, and re-layouts: 11.3 us -> 4.04 us
where the time goes in v3:
time: 199 us; the launch traced here: 197 us
  Pallas kernels  192 us (96%)
  local copies, waits for them, and re-layouts  4.04 us (2%)
    pallas_call x1, Pallas kernels, on_device(): pl.pallas_call(functools.partial(kernel, n_samp, n_bin), out_shape=(pltpu...  192 us
    unnamed x2, local copies, waits for them, and re-layouts  4.04 us

profile of v3, /device:TPU:0, one launch (start us, length us, event | category | flops | bytes accessed | tf_op | source)
XLA Modules:
  0.0 196.7 jit_solution(14332646809622258665)
XLA Ops:
  0.6 192.1 %denoise.1 = (bf16[1024,4096]{1,0:T(8,128)(2,1)S(1)}, f32[20,1024]{1,0:T(8,128)S(1)}) custom-call(bf16[8192,512]{1,0:T(8,128)(2,1)} %x_ref.1, f32[1,4096]{1,0:T(1,128)} %bitcast.4, f32[1,4096]{1,0:T(1,128)} %bitcast.5, f32[33]{0:T(128)} %taps_ref.1, bf16[20,512]{1,0:T(8,128)(2,1)} %load_ref.1), custom_call_target="tpu_custom_call" | custom-call | tf_op jit(solution)/shard_map/denoise/pallas_call | solution.py:347
  192.7 3.4 %copy.9 = bf16[1024,4096]{1,0:T(8,128)(2,1)} copy(bf16[1024,4096]{1,0:T(8,128)(2,1)S(1)} %get-tuple-element.6) | data formatting | bytes 16777216
  196.1 0.6 copy.10

commit v4 on v3

--- a/solution.py
+++ b/solution.py
@@ -13,6 +13,7 @@
 WIN = OUT + 2 * EDGE
 CHUNK = 128
 AHEAD = 3
+TAIL = ((0, 64), (64, 32), (96, 32))
 EPS = 1e-05
 MESH = pl.DeviceIdType.MESH
 F32 = jnp.float32
@@ -35,7 +36,7 @@
     n_samp, n_bin, x_ref, gc_ref, map_ref, taps_ref, load_ref, z_ref, scores_ref,
     land, xbuf, toeplitz, band, wpad, mrows, mean, part, parts, total, totals,
     lpad, lparts, lall, lstack, cent, resid,
-    local_sem, x_sem, send_sem, recv_sem, lsend, lrecv, ssend, srecv, psend, precv, tsend, trecv,
+    local_sem, x_sem, send_sem, recv_sem, tail_send, tail_recv, lsend, lrecv, ssend, srecv, psend, precv, tsend, trecv,
 ):
     rows, width = x_ref.shape
     share = rows // n_bin
@@ -117,6 +118,23 @@
             device_id={"bin": to}, device_id_type=MESH,
         )
 
+    def tail_copy(index, step, owner):
+        to = lax.rem(me + step, n_bin)
+        offset, size = TAIL[index]
+        offset = offset + share - CHUNK
+        start = pl.multiple_of(to * share + offset, size)
+        return pltpu.make_async_remote_copy(
+            src_ref=x_ref.at[pl.ds(start, size), :],
+            dst_ref=land.at[pl.ds(offset, size), landed(owner)],
+            send_sem=tail_send.at[index, step - 1], recv_sem=tail_recv.at[index, step - 1],
+            device_id={"bin": to}, device_id_type=MESH,
+        )
+
+    def send_tail():
+        for index in range(len(TAIL)):
+            for step in order:
+                tail_copy(index, step, me).start()
+
     def part_copy(step, owner):
         return pltpu.make_async_remote_copy(
             src_ref=part, dst_ref=parts.at[owner],
@@ -259,66 +277,83 @@
             folded = folded + value[:, k * 128:(k + 1) * 128]
         return folded
 
-    def finish(chunk, carry):
-        base = pl.multiple_of(chunk * CHUNK, CHUNK)
-        for step in order:
-            block_copy(chunk, step, bin_source(step)).wait_recv()
-
-        @pl.when(chunk + AHEAD < chunks)
-        def _():
-            send_chunk(chunk + AHEAD)
+    def finish_rows(base, size, unroll):
+        rows_at = pl.ds(base, size)
+        local = pl.ds(0, size)
 
         def smooth_block(j, carry):
             start = pl.multiple_of(j * OUT, OUT)
-            value = smooth(land[pl.ds(base, CHUNK), pl.ds(start, WIN)], j)
-            cent[:, pl.ds(start, OUT)] = (
+            value = smooth(land[rows_at, pl.ds(start, WIN)], j)
+            cent[local, pl.ds(start, OUT)] = (
                 value - mean[pl.ds(0, 1), pl.ds(start, OUT)]
             ).astype(BF16)
             return carry
 
-        lax.fori_loop(0, blocks, smooth_block, 0, unroll=2)
+        lax.fori_loop(0, blocks, smooth_block, 0, unroll=unroll)
         score = lax.dot_general(
-            cent[...], lall[...], (((1,), (1,)), ((), ())), preferred_element_type=F32
-        )
-        scores_ref[:, pl.ds(base, CHUNK)] = jnp.transpose(score)[0:comps, :]
+            cent[local, :], lall[...], (((1,), (1,)), ((), ())), preferred_element_type=F32
+        )
+        scores_ref[:, rows_at] = jnp.transpose(score)[0:comps, :]
         pieces3 = jnp.concatenate(split3(score), axis=1)
 
         def residual_block(j, acc):
             cols = pl.ds(pl.multiple_of(j * OUT, OUT), OUT)
-            value = cent[:, cols].astype(F32) - jnp.dot(
+            value = cent[local, cols].astype(F32) - jnp.dot(
                 pieces3, lstack[:, cols], preferred_element_type=F32
             )
-            resid[:, cols] = value
+            resid[local, cols] = value
             return acc + lanes(value)
 
-        zero = jnp.zeros((CHUNK, 128), F32)
-        acc = lax.fori_loop(0, blocks, residual_block, zero, unroll=2)
+        zero = jnp.zeros((size, 128), F32)
+        acc = lax.fori_loop(0, blocks, residual_block, zero, unroll=unroll)
         row_mean = jnp.sum(acc, axis=1, keepdims=True) / bins
 
         def square_block(j, acc):
             cols = pl.ds(pl.multiple_of(j * OUT, OUT), OUT)
-            shifted = resid[:, cols] - row_mean
+            shifted = resid[local, cols] - row_mean
             return acc + lanes(shifted * shifted)
 
-        acc = lax.fori_loop(0, blocks, square_block, zero, unroll=2)
+        acc = lax.fori_loop(0, blocks, square_block, zero, unroll=unroll)
         scale = 1.0 / jnp.sqrt(jnp.sum(acc, axis=1, keepdims=True) / bins + EPS)
 
         def store_block(j, carry):
             cols = pl.ds(pl.multiple_of(j * OUT, OUT), OUT)
-            z_ref[pl.ds(base, CHUNK), cols] = ((resid[:, cols] - row_mean) * scale).astype(BF16)
+            z_ref[rows_at, cols] = ((resid[local, cols] - row_mean) * scale).astype(BF16)
             return carry
 
-        lax.fori_loop(0, blocks, store_block, 0, unroll=2)
+        lax.fori_loop(0, blocks, store_block, 0, unroll=unroll)
+
+    def finish(chunk, carry):
+        for step in order:
+            block_copy(chunk, step, bin_source(step)).wait_recv()
+
+        @pl.when(chunk + AHEAD < chunks - 1)
+        def _():
+            send_chunk(chunk + AHEAD)
+
+        @pl.when(chunk + AHEAD == chunks - 1)
+        def _():
+            send_tail()
+
+        finish_rows(pl.multiple_of(chunk * CHUNK, CHUNK), CHUNK, 2)
         return carry
 
-    lax.fori_loop(0, chunks, finish, 0)
+    assert chunks > AHEAD
+    lax.fori_loop(0, chunks - 1, finish, 0)
+    for index, (offset, size) in enumerate(TAIL):
+        for step in order:
+            tail_copy(index, step, bin_source(step)).wait_recv()
+        finish_rows(share - CHUNK + offset, size, 4)
 
     def drain(chunk, carry):
         for step in order:
             block_copy(chunk, step, me).wait_send()
         return carry
 
-    lax.fori_loop(0, chunks, drain, 0)
+    lax.fori_loop(0, chunks - 1, drain, 0)
+    for index in range(len(TAIL)):
+        for step in order:
+            tail_copy(index, step, me).wait_send()
     for step in order:
         total_copy(step, me).wait_send()
 
@@ -374,6 +409,8 @@
             dma((8,)),
             dma((chunks, n_bin - 1)),
             dma((chunks, n_bin - 1)),
+            dma((len(TAIL), n_bin - 1)),
+            dma((len(TAIL), n_bin - 1)),
             dma((n_bin - 1,)),
             dma((n_bin - 1,)),
             dma((n_samp - 1,)),

time: 199 us -> 200 us (level)
  Pallas kernels: 192 us -> 195 us
    pallas_call x1, Pallas kernels: 192 us -> 195 us  [on_device(): pl.pallas_call(functools.partial(kernel, n_samp, n_bin), out_shape=(pltpu...]
where the time goes in v4:
time: 200 us; the launch traced here: 199 us
  Pallas kernels  195 us (98%)
  local copies, waits for them, and re-layouts  4.04 us (2%)
    pallas_call x1, Pallas kernels, on_device(): pl.pallas_call(functools.partial(kernel, n_samp, n_bin), out_shape=(pltpu...  195 us
    unnamed x2, local copies, waits for them, and re-layouts  4.04 us

profile of v4, /device:TPU:0, one launch (start us, length us, event | category | flops | bytes accessed | tf_op | source)
XLA Modules:
  0.0 199.5 jit_solution(7312485171840135679)
XLA Ops:
  0.6 194.8 %denoise.1 = (bf16[1024,4096]{1,0:T(8,128)(2,1)S(1)}, f32[20,1024]{1,0:T(8,128)S(1)}) custom-call(bf16[8192,512]{1,0:T(8,128)(2,1)} %x_ref.1, f32[1,4096]{1,0:T(1,128)} %bitcast.4, f32[1,4096]{1,0:T(1,128)} %bitcast.5, f32[33]{0:T(128)} %taps_ref.1, bf16[20,512]{1,0:T(8,128)(2,1)} %load_ref.1), custom_call_target="tpu_custom_call" | custom-call | tf_op jit(solution)/shard_map/denoise/pallas_call | solution.py:382
  195.4 3.4 %copy.9 = bf16[1024,4096]{1,0:T(8,128)(2,1)} copy(bf16[1024,4096]{1,0:T(8,128)(2,1)S(1)} %get-tuple-element.6) | data formatting | bytes 16777216
  198.8 0.6 copy.10

commit v5 on v4

--- a/solution.py
+++ b/solution.py
@@ -12,7 +12,7 @@
 OUT = 256
 WIN = OUT + 2 * EDGE
 CHUNK = 128
-AHEAD = 3
+AHEAD = 6
 TAIL = ((0, 64), (64, 32), (96, 32))
 EPS = 1e-05
 MESH = pl.DeviceIdType.MESH
@@ -42,6 +42,7 @@
     share = rows // n_bin
     bins = width * n_bin
     chunks = share // CHUNK
+    ahead = min(AHEAD, chunks - 1)
     blocks = bins // OUT
     comps = load_ref.shape[0]
     kpad = lpad.shape[0]
@@ -218,7 +219,7 @@
     for step in order:
         total_copy(step, me).start()
     totals[:, columns(me)] = total[...]
-    for chunk in range(first, min(AHEAD, chunks)):
+    for chunk in range(first, ahead):
         send_chunk(chunk)
 
     @pl.when(samp < lgroups)
@@ -327,18 +328,18 @@
         for step in order:
             block_copy(chunk, step, bin_source(step)).wait_recv()
 
-        @pl.when(chunk + AHEAD < chunks - 1)
+        @pl.when(chunk + ahead < chunks - 1)
         def _():
-            send_chunk(chunk + AHEAD)
-
-        @pl.when(chunk + AHEAD == chunks - 1)
+            send_chunk(chunk + ahead)
+
+        @pl.when(chunk + ahead == chunks - 1)
         def _():
             send_tail()
 
         finish_rows(pl.multiple_of(chunk * CHUNK, CHUNK), CHUNK, 2)
         return carry
 
-    assert chunks > AHEAD
+    assert ahead >= first
     lax.fori_loop(0, chunks - 1, finish, 0)
     for index, (offset, size) in enumerate(TAIL):
         for step in order:

time: 200 us -> 200 us (level)
  no operation moved by 1% of the time
where the time goes in v5:
time: 200 us; the launch traced here: 199 us
  Pallas kernels  195 us (98%)
  local copies, waits for them, and re-layouts  4.04 us (2%)
    pallas_call x1, Pallas kernels, on_device(): pl.pallas_call(functools.partial(kernel, n_samp, n_bin), out_shape=(pltpu...  195 us
    unnamed x2, local copies, waits for them, and re-layouts  4.04 us

profile of v5, /device:TPU:0, one launch (start us, length us, event | category | flops | bytes accessed | tf_op | source)
XLA Modules:
  0.0 199.5 jit_solution(17439202220238536223)
XLA Ops:
  0.6 194.8 %denoise.1 = (bf16[1024,4096]{1,0:T(8,128)(2,1)S(1)}, f32[20,1024]{1,0:T(8,128)S(1)}) custom-call(bf16[8192,512]{1,0:T(8,128)(2,1)} %x_ref.1, f32[1,4096]{1,0:T(1,128)} %bitcast.4, f32[1,4096]{1,0:T(1,128)} %bitcast.5, f32[33]{0:T(128)} %taps_ref.1, bf16[20,512]{1,0:T(8,128)(2,1)} %load_ref.1), custom_call_target="tpu_custom_call" | custom-call | tf_op jit(solution)/shard_map/denoise/pallas_call | solution.py:383
  195.4 3.4 %copy.9 = bf16[1024,4096]{1,0:T(8,128)(2,1)} copy(bf16[1024,4096]{1,0:T(8,128)(2,1)S(1)} %get-tuple-element.6) | data formatting | bytes 16777216
  198.8 0.6 copy.10
